TPU v7x, 32 devices: a whole 2x2x4 slice. The times are simulated.
32 devices in a mesh: dp: 4 (over y, x), fsdp: 8 (over z, core).
Axes of the slice: x: 2, y: 2, z: 4, core: 2. Of those that a mesh axis runs over, the one named last changes fastest.
Arguments:
- scenes_in: bfloat16 [32, 256, 1024], P(('dp', 'fsdp')), may hold values from -6 to 6
- scene_lengths: int32 [32], P(('dp', 'fsdp')), may hold values from 128 to 256, as said below
- cotangent: bfloat16 [32, 256, 1024], P(('dp', 'fsdp')), may hold values from -6 to 6
- qkv_weight: bfloat16 [1024, 3072], P('fsdp'), may hold values from -0.1875 to 0.1875
- out_weight: bfloat16 [1024, 1024], P('fsdp'), may hold values from -0.75 to 0.75
- up_weight: bfloat16 [1024, 4096], P('fsdp'), may hold values from -0.1875 to 0.1875
- down_weight: bfloat16 [4096, 1024], P('fsdp'), may hold values from -0.125 to 0.125
- gain_one: bfloat16 [1024], P('fsdp'), may hold values from 0.5 to 1.5
- bias_one: bfloat16 [1024], P('fsdp'), may hold values from -2 to 2
- gain_two: bfloat16 [1024], P('fsdp'), may hold values from 0.5 to 1.5
- bias_two: bfloat16 [1024], P('fsdp'), may hold values from -2 to 2
Outputs:
- layer_out: bfloat16 [32, 256, 1024], P(('dp', 'fsdp'))
- input_grad: bfloat16 [32, 256, 1024], P(('dp', 'fsdp'))
- qkv_grad: float32 [1024, 3072], P('fsdp')
- out_grad: float32 [1024, 1024], P('fsdp')
- up_grad: float32 [1024, 4096], P('fsdp')
- down_grad: float32 [4096, 1024], P('fsdp')
- gain_one_grad: float32 [1024], P('fsdp')
- bias_one_grad: float32 [1024], P('fsdp')
- gain_two_grad: float32 [1024], P('fsdp')
- bias_two_grad: float32 [1024], P('fsdp')
Inputs may be any that keep to these rules, and one draw needn't show every extreme that they name: `scene_lengths`: each length is a multiple of 128; some scene has exactly 256 tokens.
All inputs are finite; a program needn't handle non-finite values.
Results may differ from a plain program's by a relative error of at most 0.017.
Values may be sent and summed in bfloat16 or wider, within the bound.
A program may use at most 192 MiB of HBM per device.

v0:
```python
import math
import jax
import jax.numpy as jnp
from jax import lax
from jax.sharding import PartitionSpec as P

D = 1024
HEADS = 16
HEAD_DIM = 64
epsilon = 1e-05


def norm_rows(values_in):
    row_mean = jnp.mean(values_in, axis=-1, keepdims=True)
    centered = values_in - row_mean
    variance = jnp.mean(centered * centered, axis=-1, keepdims=True)
    inverse = lax.rsqrt(variance + epsilon)
    return (centered * inverse, inverse)


def norm_back(grad_normed, normed, inverse):
    first_mean = jnp.mean(grad_normed, axis=-1, keepdims=True)
    second_mean = jnp.mean(grad_normed * normed, axis=-1, keepdims=True)
    return inverse * (grad_normed - first_mean - normed * second_mean)


def inner_rows(left, right):
    return lax.dot_general(
        left, right, (((0,), (0,)), ((), ())), preferred_element_type=jnp.float32
    )


def outer_cols(left, right):
    return lax.dot_general(
        left, right, (((1,), (1,)), ((), ())), preferred_element_type=jnp.float32
    )


def forward_pass(inputs, key_valid, params):
    qkv_weight, out_weight, up_weight, down_weight, gain_one, bias_one, gain_two, bias_two = params
    seq_len = inputs.shape[0]
    normed_one, inverse_one = norm_rows(inputs)
    hidden_one = (normed_one * gain_one.astype(jnp.float32) + bias_one.astype(jnp.float32)).astype(
        jnp.bfloat16
    )
    qkv_low = jnp.dot(hidden_one, qkv_weight, preferred_element_type=jnp.float32).astype(
        jnp.bfloat16
    )
    split_view = qkv_low.reshape(seq_len, 3, HEADS, HEAD_DIM)
    queries = split_view[:, 0]
    keys_all = split_view[:, 1]
    values_all = split_view[:, 2]
    scale_factor = 1.0 / math.sqrt(HEAD_DIM)
    scores = (
        jnp.einsum("qhd,khd->hqk", queries, keys_all, preferred_element_type=jnp.float32)
        * scale_factor
    )
    masked = jnp.where(key_valid[None, None, :], scores, -1e30)
    highest = jnp.max(masked, axis=-1, keepdims=True)
    expont = jnp.exp(masked - highest)
    probs = expont / jnp.sum(expont, axis=-1, keepdims=True)
    probs_low = probs.astype(jnp.bfloat16)
    attended = jnp.einsum("hqk,khd->qhd", probs_low, values_all, preferred_element_type=jnp.float32)
    attn_low = attended.reshape(seq_len, D).astype(jnp.bfloat16)
    resid_one = inputs + jnp.dot(attn_low, out_weight, preferred_element_type=jnp.float32)
    normed_two, inverse_two = norm_rows(resid_one)
    hidden_two = (normed_two * gain_two.astype(jnp.float32) + bias_two.astype(jnp.float32)).astype(
        jnp.bfloat16
    )
    hidden_pre = jnp.dot(hidden_two, up_weight, preferred_element_type=jnp.float32)
    activated = jax.nn.gelu(hidden_pre, approximate=False).astype(jnp.bfloat16)
    result = resid_one + jnp.dot(activated, down_weight, preferred_element_type=jnp.float32)
    return (
        result,
        normed_one,
        inverse_one,
        hidden_one,
        queries,
        keys_all,
        values_all,
        probs,
        probs_low,
        attn_low,
        normed_two,
        inverse_two,
        hidden_two,
        hidden_pre,
        activated,
    )


def mlp_back(grad_out, saved, params):
    up_weight, down_weight, gain_two = (params[2], params[3], params[6])
    normed_two, inverse_two, hidden_two, hidden_pre, activated = (
        saved[10],
        saved[11],
        saved[12],
        saved[13],
        saved[14],
    )
    grad_low = grad_out.astype(jnp.bfloat16)
    down_grad = inner_rows(activated, grad_low)
    grad_act = outer_cols(grad_low, down_weight)
    cumul = 0.5 * (1.0 + lax.erf(hidden_pre * (1.0 / math.sqrt(2.0))))
    density = jnp.exp(-0.5 * hidden_pre * hidden_pre) * (1.0 / math.sqrt(2.0 * math.pi))
    grad_pre = (grad_act * (cumul + hidden_pre * density)).astype(jnp.bfloat16)
    up_grad = inner_rows(hidden_two, grad_pre)
    grad_hidden = outer_cols(grad_pre, up_weight)
    gain_two_grad = jnp.sum(grad_hidden * normed_two, axis=0)
    bias_two_grad = jnp.sum(grad_hidden, axis=0)
    grad_resid = grad_out + norm_back(
        grad_hidden * gain_two.astype(jnp.float32), normed_two, inverse_two
    )
    return (grad_resid, up_grad, down_grad, gain_two_grad, bias_two_grad)


def attn_back(grad_resid, saved, params):
    qkv_weight, out_weight, gain_one = (params[0], params[1], params[4])
    normed_one, inverse_one, hidden_one = (saved[1], saved[2], saved[3])
    queries, keys_all, values_all, probs, probs_low, attn_low = (
        saved[4],
        saved[5],
        saved[6],
        saved[7],
        saved[8],
        saved[9],
    )
    seq_len = grad_resid.shape[0]
    scale_factor = 1.0 / math.sqrt(HEAD_DIM)
    resid_low = grad_resid.astype(jnp.bfloat16)
    out_grad = inner_rows(attn_low, resid_low)
    grad_attn = (
        outer_cols(resid_low, out_weight).astype(jnp.bfloat16).reshape(seq_len, HEADS, HEAD_DIM)
    )
    grad_probs = jnp.einsum(
        "qhd,khd->hqk", grad_attn, values_all, preferred_element_type=jnp.float32
    )
    row_dot = jnp.sum(probs * grad_probs, axis=-1, keepdims=True)
    grad_scores = (probs * (grad_probs - row_dot)).astype(jnp.bfloat16)
    grad_values = jnp.einsum(
        "hqk,qhd->khd", probs_low, grad_attn, preferred_element_type=jnp.float32
    )
    grad_queries = (
        jnp.einsum("hqk,khd->qhd", grad_scores, keys_all, preferred_element_type=jnp.float32)
        * scale_factor
    )
    grad_keys = (
        jnp.einsum("hqk,qhd->khd", grad_scores, queries, preferred_element_type=jnp.float32)
        * scale_factor
    )
    grad_qkv = (
        jnp.stack([grad_queries, grad_keys, grad_values], axis=1)
        .reshape(seq_len, 3 * D)
        .astype(jnp.bfloat16)
    )
    qkv_grad = inner_rows(hidden_one, grad_qkv)
    grad_hidden = outer_cols(grad_qkv, qkv_weight)
    gain_one_grad = jnp.sum(grad_hidden * normed_one, axis=0)
    bias_one_grad = jnp.sum(grad_hidden, axis=0)
    input_grad = grad_resid + norm_back(
        grad_hidden * gain_one.astype(jnp.float32), normed_one, inverse_one
    )
    return (input_grad, qkv_grad, out_grad, gain_one_grad, bias_one_grad)


def on_device(
    scenes_in,
    scene_lengths,
    cotangent,
    qkv_weight,
    out_weight,
    up_weight,
    down_weight,
    gain_one,
    bias_one,
    gain_two,
    bias_two,
):
    params = (
        lax.all_gather(qkv_weight, "fsdp", axis=0, tiled=True),
        lax.all_gather(out_weight, "fsdp", axis=0, tiled=True),
        lax.all_gather(up_weight, "fsdp", axis=0, tiled=True),
        lax.all_gather(down_weight, "fsdp", axis=0, tiled=True),
        lax.all_gather(gain_one, "fsdp", axis=0, tiled=True),
        lax.all_gather(bias_one, "fsdp", axis=0, tiled=True),
        lax.all_gather(gain_two, "fsdp", axis=0, tiled=True),
        lax.all_gather(bias_two, "fsdp", axis=0, tiled=True),
    )
    inputs = scenes_in[0].astype(jnp.float32)
    seq_len = inputs.shape[0]
    positions = jnp.arange(seq_len, dtype=jnp.int32)
    key_valid = positions < scene_lengths[0]
    row_mask = key_valid.astype(jnp.float32)[:, None]
    saved = forward_pass(inputs, key_valid, params)
    layer_out = (saved[0] * row_mask).astype(jnp.bfloat16)[None]
    grad_out = cotangent[0].astype(jnp.float32) * row_mask
    params_back = (
        lax.all_gather(qkv_weight, "fsdp", axis=0, tiled=True),
        lax.all_gather(out_weight, "fsdp", axis=0, tiled=True),
        lax.all_gather(up_weight, "fsdp", axis=0, tiled=True),
        lax.all_gather(down_weight, "fsdp", axis=0, tiled=True),
        lax.all_gather(gain_one, "fsdp", axis=0, tiled=True),
        lax.all_gather(bias_one, "fsdp", axis=0, tiled=True),
        lax.all_gather(gain_two, "fsdp", axis=0, tiled=True),
        lax.all_gather(bias_two, "fsdp", axis=0, tiled=True),
    )
    saved_back = forward_pass(inputs, key_valid, params_back)
    grad_resid, up_grad, down_grad, gain_two_grad, bias_two_grad = mlp_back(
        grad_out, saved_back, params_back
    )
    input_grad, qkv_grad, out_grad, gain_one_grad, bias_one_grad = attn_back(
        grad_resid, saved_back, params_back
    )
    shares = (
        lax.psum_scatter(qkv_grad, "fsdp", scatter_dimension=0, tiled=True),
        lax.psum_scatter(out_grad, "fsdp", scatter_dimension=0, tiled=True),
        lax.psum_scatter(up_grad, "fsdp", scatter_dimension=0, tiled=True),
        lax.psum_scatter(down_grad, "fsdp", scatter_dimension=0, tiled=True),
        lax.psum_scatter(gain_one_grad, "fsdp", scatter_dimension=0, tiled=True),
        lax.psum_scatter(bias_one_grad, "fsdp", scatter_dimension=0, tiled=True),
        lax.psum_scatter(gain_two_grad, "fsdp", scatter_dimension=0, tiled=True),
        lax.psum_scatter(bias_two_grad, "fsdp", scatter_dimension=0, tiled=True),
    )
    summed = (
        lax.psum(shares[0].astype(jnp.bfloat16), "dp").astype(jnp.float32),
        lax.psum(shares[1].astype(jnp.bfloat16), "dp").astype(jnp.float32),
        lax.psum(shares[2].astype(jnp.bfloat16), "dp").astype(jnp.float32),
        lax.psum(shares[3].astype(jnp.bfloat16), "dp").astype(jnp.float32),
        lax.psum(shares[4].astype(jnp.bfloat16), "dp").astype(jnp.float32),
        lax.psum(shares[5].astype(jnp.bfloat16), "dp").astype(jnp.float32),
        lax.psum(shares[6].astype(jnp.bfloat16), "dp").astype(jnp.float32),
        lax.psum(shares[7].astype(jnp.bfloat16), "dp").astype(jnp.float32),
    )
    qkv_total, out_total, up_total, down_total = (summed[0], summed[1], summed[2], summed[3])
    gain_one_total, bias_one_total, gain_two_total, bias_two_total = (
        summed[4],
        summed[5],
        summed[6],
        summed[7],
    )
    input_out = input_grad.astype(jnp.bfloat16)[None]
    return (
        layer_out,
        input_out,
        qkv_total,
        out_total,
        up_total,
        down_total,
        gain_one_total,
        bias_one_total,
        gain_two_total,
        bias_two_total,
    )


def solution(mesh):
    placed = (
        P(("dp", "fsdp"), None, None),
        P(("dp", "fsdp")),
        P(("dp", "fsdp"), None, None),
        P("fsdp", None),
        P("fsdp", None),
        P("fsdp", None),
        P("fsdp", None),
        P("fsdp"),
        P("fsdp"),
        P("fsdp"),
        P("fsdp"),
    )
    return jax.shard_map(
        on_device,
        mesh=mesh,
        in_specs=placed,
        out_specs=(
            P(("dp", "fsdp"), None, None),
            P(("dp", "fsdp"), None, None),
            P("fsdp", None),
            P("fsdp", None),
            P("fsdp", None),
            P("fsdp", None),
            P("fsdp"),
            P("fsdp"),
            P("fsdp"),
            P("fsdp"),
        ),
        check_vma=False,
    )
```

profile of v0, /device:TPU:0, one launch (start us, length us, event | category | flops | bytes accessed | tf_op | source)
XLA Modules:
  0.0 905.0 jit_solution(12101224661716060638)
XLA Ops:
  10.0 13.6 %all-gather = bf16[8,1,128]{2,1,0:T(2,128)(2,1)S(1)} all-gather(bf16[1,1,128]{2,1,0:T(2,128)(2,1)} %bitcast.139), channel_id=1, replica_groups=mesh['dp'=4,'fsdp'=8] {'fsdp'}, dimensions={0}, use_global_device_ids=true | all-gather | bytes 2304 | tf_op jit(solution)/shard_map/all_gather | solution.py:184
  23.7 9.3 %all-gather.1 = bf16[8,1,128]{2,1,0:T(2,128)(2,1)S(1)} all-gather(bf16[1,1,128]{2,1,0:T(2,128)(2,1)} %bitcast.140), channel_id=1, replica_groups=mesh['dp'=4,'fsdp'=8] {'fsdp'}, dimensions={0}, use_global_device_ids=true | all-gather | bytes 2304 | tf_op jit(solution)/shard_map/all_gather | solution.py:185
  33.6 11.4 %all-gather.2 = bf16[8,1,128]{2,1,0:T(2,128)(2,1)S(1)} all-gather(bf16[1,1,128]{2,1,0:T(2,128)(2,1)} %bitcast.141), channel_id=1, replica_groups=mesh['dp'=4,'fsdp'=8] {'fsdp'}, dimensions={0}, use_global_device_ids=true | all-gather | bytes 2304 | tf_op jit(solution)/shard_map/all_gather | solution.py:186
  45.0 9.3 %all-gather.3 = bf16[8,1,128]{2,1,0:T(2,128)(2,1)S(1)} all-gather(bf16[1,1,128]{2,1,0:T(2,128)(2,1)} %bitcast.142), channel_id=1, replica_groups=mesh['dp'=4,'fsdp'=8] {'fsdp'}, dimensions={0}, use_global_device_ids=true | all-gather | bytes 2304 | tf_op jit(solution)/shard_map/all_gather | solution.py:187
  56.9 20.2 %all-gather.9.cloned.1.call-done = bf16[1024,3072]{1,0:T(8,128)(2,1)} async-done(((bf16[128,3072]{1,0:T(8,128)(2,1)}), bf16[1024,3072]{1,0:T(8,128)(2,1)}) %all-gather.9.cloned.1.call-update) | async-done | bytes 6291472 | tf_op jit(solution)/shard_map/all_gather | solution.py:180
  77.1 5.8 convolution_convert_fusion
  89.7 16.8 %all-gather.11.cloned.1.call-done = bf16[1024,1024]{1,0:T(8,128)(2,1)} async-done(((bf16[128,1024]{1,0:T(8,128)(2,1)}), bf16[1024,1024]{1,0:T(8,128)(2,1)}) %all-gather.11.cloned.1.call-update) | async-done | bytes 2097168 | tf_op jit(solution)/shard_map/all_gather | solution.py:181
  106.5 2.4 fusion.76
  109.2 80.4 %all-gather.13.cloned.1.call-done = bf16[1024,4096]{1,0:T(8,128)(2,1)} async-done(((bf16[128,4096]{1,0:T(8,128)(2,1)}), bf16[1024,4096]{1,0:T(8,128)(2,1)}) %all-gather.13.cloned.1.call-update) | async-done | bytes 8388624 | tf_op jit(solution)/shard_map/all_gather | solution.py:182
  189.6 15.3 %fusion.4 = (bf16[256,4096]{1,0:T(8,128)(2,1)}, f32[256,4096]{1,0:T(8,128)}) fusion(bf16[1024,4096]{1,0:T(8,128)(2,1)} %all-gather.13.cloned.1.call-done, f32[256,1024]{1,0:T(8,128)S(1)} %get-tuple-element.33, f32[1024]{0:T(1024)S(1)} %bitcast.131, f32[1024]{0:T(1024)S(1)} %bitcast.127, f32[256]{0:T(256)S(1)} %add_rsqrt_fusion, ...), kind=kOutput, calls=%fused_computation.7 | convolution fusion | flops 2216951808 | bytes 15738880 | tf_op jit(solution)/shard_map/dot_general | solution.py:70
  204.8 66.8 %all-gather.15.cloned.1.call-done = bf16[4096,1024]{1,0:T(8,128)(2,1)} async-done(((bf16[512,1024]{1,0:T(8,128)(2,1)}), bf16[4096,1024]{1,0:T(8,128)(2,1)}) %all-gather.15.cloned.1.call-update) | async-done | bytes 8388624 | tf_op jit(solution)/shard_map/all_gather | solution.py:183
  271.6 6.8 fusion.1
  278.6 2.7 multiply_reduce_fusion.1
  281.8 2.8 fusion.64
  288.0 3.8 multiply_reduce_fusion
  296.9 6.5 fusion.50
  303.8 9.9 %fusion.73 = f32[1024,4096]{1,0:T(8,128)} fusion(bf16[256,4096]{1,0:T(8,128)(2,1)} %copy-done.10, f32[256,1024]{1,0:T(8,128)S(1)} %get-tuple-element.33, f32[1024]{0:T(1024)S(1)} %bitcast.132, f32[1024]{0:T(1024)S(1)} %bitcast.130, f32[256]{0:T(256)S(1)} %add_rsqrt_fusion, f32[256]{0:T(256)S(1)} %broadcast_multiply_fusion.4), kind=kOutput, calls=%fused_computation.121 | convolution fusion | flops 2148794368 | bytes 19933184 | tf_op jit(solution)/shard_map/dot_general | solution.py:28
  314.7 9.8 %fusion.67 = f32[4096,1024]{1,0:T(8,128)} fusion(bf16[256,4096]{1,0:T(8,128)(2,1)} %get-tuple-element.34, bf16[1,256,1024]{2,1,0:T(8,128)(2,1)S(1)} %copy-done.7, f32[256]{0:T(256)S(1)} %fusion.72), kind=kOutput, calls=%fused_computation.104 | convolution fusion | flops 2148270080 | bytes 19399680 | tf_op jit(solution)/shard_map/dot_general | solution.py:28
  324.6 8.6 reduce-scatter.7.cloned.1.call-done
  334.9 128.0 %reduce-scatter.5.cloned.1.call-done = f32[128,3072]{1,0:T(8,128)} async-done(((f32[1024,3072]{1,0:T(8,128)}), f32[128,3072]{1,0:T(8,128)}) %reduce-scatter.5.cloned.1.call-update) | async-done | bytes 1572880 | tf_op jit(solution)/shard_map/reduce_scatter | solution.py:215
  465.4 166.6 %reduce-scatter.9.cloned.1.call-done = f32[128,4096]{1,0:T(8,128)} async-done(((f32[1024,4096]{1,0:T(8,128)}), f32[128,4096]{1,0:T(8,128)}) %reduce-scatter.9.cloned.1.call-update) | async-done | bytes 2097168 | tf_op jit(solution)/shard_map/reduce_scatter | solution.py:217
  632.0 2.7 convert_element_type.187
  634.7 166.3 %reduce-scatter.11.cloned.1.call-done = f32[512,1024]{1,0:T(8,128)} async-done(((f32[4096,1024]{1,0:T(8,128)}), f32[512,1024]{1,0:T(8,128)}) %reduce-scatter.11.cloned.1.call-update) | async-done | bytes 2097168 | tf_op jit(solution)/shard_map/reduce_scatter | solution.py:218
  801.0 2.7 convert_element_type.189
  805.0 6.3 fusion.39
  811.2 25.9 %all-reduce.4 = (bf16[1024]{0:T(1024)(128)(2,1)S(1)}, bf16[1024]{0:T(1024)(128)(2,1)S(1)}, bf16[1024]{0:T(1024)(128)(2,1)S(1)}, bf16[1024]{0:T(1024)(128)(2,1)S(1)}) all-reduce(f32[1024]{0:T(1024)S(1)} %get-tuple-element.12, f32[1024]{0:T(1024)S(1)} %get-tuple-element.17, ...), channel_id=6, replica_groups=mesh['dp'=4,'fsdp'=8] {'fsdp'}, use_global_device_ids=true, to_apply=%region_20.21.clone | all-reduce | flops 4096 | bytes 24576
  837.5 10.2 %all-reduce.5 = (bf16[128]{0:T(256)(128)(2,1)S(1)}, bf16[128]{0:T(256)(128)(2,1)S(1)}, bf16[128]{0:T(256)(128)(2,1)S(1)}, bf16[128]{0:T(256)(128)(2,1)S(1)}) all-reduce(bf16[128]{0:T(256)(128)(2,1)S(1)} %dynamic-slice.15, bf16[128]{0:T(256)(128)(2,1)S(1)} %dynamic-slice.14, ...), channel_id=1, replica_groups=mesh['dp'=4,'fsdp'=8] {'dp'}, use_global_device_ids=true, to_apply=%region_21.22 | all-reduce | flops 512 | bytes 2048 | tf_op jit(solution)/shard_map/psum | solution.py:229
  849.7 2.4 fusion.52
  852.2 7.8 fusion.31
  860.0 30.7 %all-reduce.9.cloned.1.call-done = (bf16[128,3072]{1,0:T(8,128)(2,1)}, bf16[128,1024]{1,0:T(8,128)(2,1)}, bf16[128,4096]{1,0:T(8,128)(2,1)}, bf16[512,1024]{1,0:T(8,128)(2,1)}) async-done(((bf16[128,3072]{1,0:T(8,128)(2,1)}, bf16[128,1024]{1,0:T(8,128)(2,1)}, bf16[128,4096]{1,0:T(8,128)(2,1)}, bf16[512,1024]{1,0:T(8,128)(2,1)}), (bf16[128,3072]{1,0:T(8,128)(2,1)}, bf16[128,1024]{1,0:T(8,128)(2,1)}, ...) | async-done | bytes 3145744 | tf_op jit(solution)/shard_map/psum | solution.py:225
  890.7 2.8 convert_element_type.188
  893.5 2.8 convert_element_type.190
  (91 shorter events, 32.0 us)
Async XLA Ops:
  7.2 69.9 %copy-start = (bf16[1,256,1024]{2,1,0:T(8,128)(2,1)S(1)}, bf16[1,256,1024]{2,1,0:T(8,128)(2,1)}, u32[]{:S(2)}) copy-start(bf16[1,256,1024]{2,1,0:T(8,128)(2,1)} %param.11) | copy-start | bytes 1572868
  7.2 69.9 %all-gather.9.cloned.1.call-start = ((), (), s32[]{:S(2)}) async-start(), calls=%async_computation.4 | async-start | bytes 7077888 | tf_op jit(solution)/shard_map/all_gather | solution.py:180
  7.9 98.6 %all-gather.11.cloned.1.call-start = ((), (), s32[]{:S(2)}) async-start(), calls=%async_computation.5 | async-start | bytes 2359296 | tf_op jit(solution)/shard_map/all_gather | solution.py:181
  8.7 180.9 %all-gather.13.cloned.1.call-start = ((), (), s32[]{:S(2)}) async-start(), calls=%async_computation.6 | async-start | bytes 9437184 | tf_op jit(solution)/shard_map/all_gather | solution.py:182
  9.4 262.2 %all-gather.15.cloned.1.call-start = ((), (), s32[]{:S(2)}) async-start(), calls=%async_computation.7 | async-start | bytes 9437184 | tf_op jit(solution)/shard_map/all_gather | solution.py:183
  10.0 323.2 %reduce-scatter.7.cloned.1.call-start = ((), (), s32[]{:S(2)}) async-start(), calls=%async_computation.9 | async-start | bytes 4718592 | tf_op jit(solution)/shard_map/reduce_scatter | solution.py:216
  84.7 2.5 copy-start.1
  87.2 2.0 copy-start.4
  89.6 115.2 %copy-start.8 = (bf16[16,64,256]{2,1,0:T(8,128)(2,1)}, bf16[16,64,256]{2,1,0:T(8,128)(2,1)S(1)}, u32[]{:S(2)}) copy-start(bf16[16,64,256]{2,1,0:T(8,128)(2,1)S(1)} %convolution_convert_fusion.2) | copy-start | bytes 1572868
  189.6 82.0 %copy-start.6 = (bf16[1,256,1024]{2,1,0:T(8,128)(2,1)S(1)}, bf16[1,256,1024]{2,1,0:T(8,128)(2,1)}, u32[]{:S(2)}) copy-start(bf16[1,256,1024]{2,1,0:T(8,128)(2,1)} %param.13) | copy-start | bytes 1572868
  271.6 7.0 copy-start.14
  278.6 2.7 copy-start.10
  278.6 3.1 copy-start.9
  284.6 178.4 %reduce-scatter.5.cloned.1.call-start = ((), (), s32[]{:S(2)}) async-start(), calls=%async_computation.8 | async-start | bytes 14155776 | tf_op jit(solution)/shard_map/reduce_scatter | solution.py:215
  288.0 4.1 copy-start.5
  292.1 1.4 copy-start.2
  293.5 1.2 copy-start.12
  295.8 1.1 copy-start.3
  303.5 328.5 %reduce-scatter.9.cloned.1.call-start = ((), (), s32[]{:S(2)}) async-start(), calls=%async_computation.10 | async-start | bytes 18874368 | tf_op jit(solution)/shard_map/reduce_scatter | solution.py:217
  313.7 1.0 copy-start.7
  313.7 487.3 %reduce-scatter.11.cloned.1.call-start = ((), (), s32[]{:S(2)}) async-start(), calls=%async_computation.11 | async-start | bytes 18874368 | tf_op jit(solution)/shard_map/reduce_scatter | solution.py:218
  324.6 566.1 %all-reduce.9.cloned.1.call-start = ((), (), s32[]{:S(2)}) async-start(), calls=%async_computation.12 | async-start | bytes 6291456 | tf_op jit(solution)/shard_map/psum | solution.py:225
  465.4 338.4 %copy-start.15 = (u32[32]{0:T(128)S(1)}, u32[32]{0:T(128)}, u32[]{:S(2)}) copy-start(u32[32]{0:T(128)} %constant.89) | copy-start | bytes 388
  890.7 5.6 copy-start.11
  890.7 6.9 copy-start.13
Sparse Core Ops, SparseCore 0:
  9.6 67.4 all-gather.8
  78.7 27.7 all-gather.10
  108.1 81.4 all-gather.12
  191.0 80.5 all-gather.14
  284.7 48.4 reduce-scatter.6
  335.3 127.5 reduce-scatter.4
  465.3 166.6 reduce-scatter.8
  634.3 166.6 reduce-scatter.10
  804.9 85.7 all-reduce.8
where the time goes:
time: 906 us; the launch traced here: 905 us
  waiting for transfers between devices  687 us (76%)
  matrix products  85.6 us (9%)
  blocking collectives  79.8 us (9%)
  other arithmetic  27.9 us (3%)
  between operations  15.4 us (2%)
    reduce_scatter x1, waiting for transfers between devices, on_device(): lax.psum_scatter(up_grad, 'fsdp', scatter_dimension=0, tiled=True)  167 us
    reduce_scatter x1, waiting for transfers between devices, on_device(): lax.psum_scatter(down_grad, 'fsdp', scatter_dimension=0, tiled=True)  166 us
    reduce_scatter x1, waiting for transfers between devices, on_device(): lax.psum_scatter(qkv_grad, 'fsdp', scatter_dimension=0, tiled=True)  128 us
    all_gather x1, waiting for transfers between devices, on_device(): lax.all_gather(up_weight, 'fsdp', axis=0, tiled=True)  80.4 us
    all_gather x1, waiting for transfers between devices, on_device(): lax.all_gather(down_weight, 'fsdp', axis=0, tiled=True)  66.8 us
    psum x1, waiting for transfers between devices, on_device(): lax.psum(shares[0].astype(jnp.bfloat16), 'dp').astype(jnp.float32)  30.7 us
    dot_general x4, matrix products, inner_rows(): lax.dot_general(left, right, (((0,), (0,)), ((), ())), preferred_element_...  29.1 us
    unnamed x1, blocking collectives  25.9 us
  transfers between devices with their start and end apart: 9, of which 9 were waited for; matrix products, arithmetic and copies ran while one was open for 10% of the time, Pallas kernels for 0%

commit v1 on v0

--- a/solution.py
+++ b/solution.py
@@ -222,7 +222,7 @@
         lax.psum_scatter(bias_two_grad, "fsdp", scatter_dimension=0, tiled=True),
     )
     summed = (
-        lax.psum(shares[0].astype(jnp.bfloat16), "dp").astype(jnp.float32),
+        jnp.sum(lax.all_gather(shares[0].astype(jnp.bfloat16), "dp"), axis=0).astype(jnp.float32),
         lax.psum(shares[1].astype(jnp.bfloat16), "dp").astype(jnp.float32),
         lax.psum(shares[2].astype(jnp.bfloat16), "dp").astype(jnp.float32),
         lax.psum(shares[3].astype(jnp.bfloat16), "dp").astype(jnp.float32),

time: 906 us -> 951 us (1.050)
  waiting for transfers between devices: 687 us -> 730 us
    reduce_scatter x1, waiting for transfers between devices: 8.55 us -> 48.1 us  [on_device(): lax.psum_scatter(out_grad, 'fsdp', scatter_dimension=0, tiled=True)]
    psum x1, waiting for transfers between devices: 30.7 us -> 59.2 us  [on_device(): lax.psum(shares[1].astype(jnp.bfloat16), 'dp').astype(jnp.float32)]
    reduce_scatter x1, waiting for transfers between devices: 128 us -> 102 us  [on_device(): lax.psum_scatter(qkv_grad, 'fsdp', scatter_dimension=0, tiled=True)]
  transfers between devices with their start and end apart: 9 -> 10, of which waited for: 9 -> 9; matrix products, arithmetic and copies ran while one was open for 10% -> 9% of each run, Pallas kernels for 0% -> 0%
where the time goes in v1:
time: 951 us; the launch traced here: 950 us
  waiting for transfers between devices  730 us (77%)
  matrix products  84.2 us (9%)
  blocking collectives  79.6 us (8%)
  other arithmetic  30.4 us (3%)
  between operations  15.7 us (2%)
  local copies, waits for them, and re-layouts  9.68 us (1%)
    reduce_scatter x1, waiting for transfers between devices, on_device(): lax.psum_scatter(up_grad, 'fsdp', scatter_dimension=0, tiled=True)  167 us
    reduce_scatter x1, waiting for transfers between devices, on_device(): lax.psum_scatter(down_grad, 'fsdp', scatter_dimension=0, tiled=True)  166 us
    reduce_scatter x1, waiting for transfers between devices, on_device(): lax.psum_scatter(qkv_grad, 'fsdp', scatter_dimension=0, tiled=True)  102 us
    all_gather x1, waiting for transfers between devices, on_device(): lax.all_gather(up_weight, 'fsdp', axis=0, tiled=True)  80.4 us
    all_gather x1, waiting for transfers between devices, on_device(): lax.all_gather(down_weight, 'fsdp', axis=0, tiled=True)  66.8 us
    psum x1, waiting for transfers between devices, on_device(): lax.psum(shares[1].astype(jnp.bfloat16), 'dp').astype(jnp.float32)  59.2 us
    reduce_scatter x1, waiting for transfers between devices, on_device(): lax.psum_scatter(out_grad, 'fsdp', scatter_dimension=0, tiled=True)  48.1 us
    dot_general x4, matrix products, inner_rows(): lax.dot_general(left, right, (((0,), (0,)), ((), ())), preferred_element_...  29.4 us
  transfers between devices with their start and end apart: 10, of which 9 were waited for; matrix products, arithmetic and copies ran while one was open for 9% of the time, Pallas kernels for 0%

profile of v1, /device:TPU:0, one launch (start us, length us, event | category | flops | bytes accessed | tf_op | source)
XLA Modules:
  0.0 950.5 jit_solution(619713570947713279)
XLA Ops:
  10.0 13.6 %all-gather.1 = bf16[8,1,128]{2,1,0:T(2,128)(2,1)S(1)} all-gather(bf16[1,1,128]{2,1,0:T(2,128)(2,1)} %bitcast.141), channel_id=1, replica_groups=mesh['dp'=4,'fsdp'=8] {'fsdp'}, dimensions={0}, use_global_device_ids=true | all-gather | bytes 2304 | tf_op jit(solution)/shard_map/all_gather | solution.py:184
  23.7 9.3 all-gather.2
  33.6 11.4 %all-gather.3 = bf16[8,1,128]{2,1,0:T(2,128)(2,1)S(1)} all-gather(bf16[1,1,128]{2,1,0:T(2,128)(2,1)} %bitcast.143), channel_id=1, replica_groups=mesh['dp'=4,'fsdp'=8] {'fsdp'}, dimensions={0}, use_global_device_ids=true | all-gather | bytes 2304 | tf_op jit(solution)/shard_map/all_gather | solution.py:186
  45.0 9.3 all-gather.4
  56.9 20.2 %all-gather.11.cloned.1.call-done = bf16[1024,3072]{1,0:T(8,128)(2,1)} async-done(((bf16[128,3072]{1,0:T(8,128)(2,1)}), bf16[1024,3072]{1,0:T(8,128)(2,1)}) %all-gather.11.cloned.1.call-update) | async-done | bytes 6291472 | tf_op jit(solution)/shard_map/all_gather | solution.py:180
  77.1 5.8 convolution_convert_fusion
  89.7 16.8 %all-gather.13.cloned.1.call-done = bf16[1024,1024]{1,0:T(8,128)(2,1)} async-done(((bf16[128,1024]{1,0:T(8,128)(2,1)}), bf16[1024,1024]{1,0:T(8,128)(2,1)}) %all-gather.13.cloned.1.call-update) | async-done | bytes 2097168 | tf_op jit(solution)/shard_map/all_gather | solution.py:181
  109.2 80.4 %all-gather.15.cloned.1.call-done = bf16[1024,4096]{1,0:T(8,128)(2,1)} async-done(((bf16[128,4096]{1,0:T(8,128)(2,1)}), bf16[1024,4096]{1,0:T(8,128)(2,1)}) %all-gather.15.cloned.1.call-update) | async-done | bytes 8388624 | tf_op jit(solution)/shard_map/all_gather | solution.py:182
  189.6 15.3 %fusion.4 = (bf16[256,4096]{1,0:T(8,128)(2,1)}, f32[256,4096]{1,0:T(8,128)}) fusion(bf16[1024,4096]{1,0:T(8,128)(2,1)} %all-gather.15.cloned.1.call-done, f32[256,1024]{1,0:T(8,128)S(1)} %get-tuple-element.32, f32[1024]{0:T(1024)S(1)} %bitcast.133, f32[1024]{0:T(1024)S(1)} %bitcast.129, f32[256]{0:T(256)S(1)} %add_rsqrt_fusion, ...), kind=kOutput, calls=%fused_computation.7 | convolution fusion | flops 2216951808 | bytes 15738880 | tf_op jit(solution)/shard_map/dot_general | solution.py:70
  204.8 66.8 %all-gather.17.cloned.1.call-done = bf16[4096,1024]{1,0:T(8,128)(2,1)} async-done(((bf16[512,1024]{1,0:T(8,128)(2,1)}), bf16[4096,1024]{1,0:T(8,128)(2,1)}) %all-gather.17.cloned.1.call-update) | async-done | bytes 8388624 | tf_op jit(solution)/shard_map/all_gather | solution.py:183
  271.6 6.8 fusion.1
  278.6 2.7 multiply_reduce_fusion.1
  283.5 3.5 multiply_reduce_fusion
  292.0 6.5 fusion.50
  299.6 2.8 fusion.64
  302.8 10.3 %fusion.73 = f32[1024,4096]{1,0:T(8,128)} fusion(bf16[256,4096]{1,0:T(8,128)(2,1)} %copy-done.11, f32[256,1024]{1,0:T(8,128)S(1)} %get-tuple-element.32, f32[1024]{0:T(1024)S(1)} %bitcast.134, f32[1024]{0:T(1024)S(1)} %bitcast.132, f32[256]{0:T(256)S(1)} %add_rsqrt_fusion, f32[256]{0:T(256)S(1)} %broadcast_multiply_fusion.4), kind=kOutput, calls=%fused_computation.121 | convolution fusion | flops 2148794368 | bytes 19933184 | tf_op jit(solution)/shard_map/dot_general | solution.py:28
  314.1 9.7 %fusion.67 = f32[4096,1024]{1,0:T(8,128)} fusion(bf16[256,4096]{1,0:T(8,128)(2,1)} %get-tuple-element.33, bf16[1,256,1024]{2,1,0:T(8,128)(2,1)S(1)} %copy-done.8, f32[256]{0:T(256)S(1)} %fusion.72), kind=kOutput, calls=%fused_computation.104 | convolution fusion | flops 2148270080 | bytes 19399680 | tf_op jit(solution)/shard_map/dot_general | solution.py:28
  323.9 102.5 %reduce-scatter.5.cloned.1.call-done = f32[128,3072]{1,0:T(8,128)} async-done(((f32[1024,3072]{1,0:T(8,128)}), f32[128,3072]{1,0:T(8,128)}) %reduce-scatter.5.cloned.1.call-update) | async-done | bytes 1572880 | tf_op jit(solution)/shard_map/reduce_scatter | solution.py:215
  428.8 48.1 %reduce-scatter.7.cloned.1.call-done = f32[128,1024]{1,0:T(8,128)} async-done(((f32[1024,1024]{1,0:T(8,128)}), f32[128,1024]{1,0:T(8,128)}) %reduce-scatter.7.cloned.1.call-update) | async-done | bytes 524304 | tf_op jit(solution)/shard_map/reduce_scatter | solution.py:216
  478.7 167.3 %reduce-scatter.9.cloned.1.call-done = f32[128,4096]{1,0:T(8,128)} async-done(((f32[1024,4096]{1,0:T(8,128)}), f32[128,4096]{1,0:T(8,128)}) %reduce-scatter.9.cloned.1.call-update) | async-done | bytes 2097168 | tf_op jit(solution)/shard_map/reduce_scatter | solution.py:217
  646.0 2.7 convert_element_type.189
  648.7 166.3 %reduce-scatter.11.cloned.1.call-done = f32[512,1024]{1,0:T(8,128)} async-done(((f32[4096,1024]{1,0:T(8,128)}), f32[512,1024]{1,0:T(8,128)}) %reduce-scatter.11.cloned.1.call-update) | async-done | bytes 2097168 | tf_op jit(solution)/shard_map/reduce_scatter | solution.py:218
  815.0 2.7 convert_element_type.191
  819.0 6.4 fusion.39
  825.4 25.9 %all-reduce.4 = (bf16[1024]{0:T(1024)(128)(2,1)S(1)}, bf16[1024]{0:T(1024)(128)(2,1)S(1)}, bf16[1024]{0:T(1024)(128)(2,1)S(1)}, bf16[1024]{0:T(1024)(128)(2,1)S(1)}) all-reduce(f32[1024]{0:T(1024)S(1)} %get-tuple-element.12, f32[1024]{0:T(1024)S(1)} %get-tuple-element.17, ...), channel_id=7, replica_groups=mesh['dp'=4,'fsdp'=8] {'fsdp'}, use_global_device_ids=true, to_apply=%region_20.21.clone | all-reduce | flops 4096 | bytes 24576
  851.7 10.0 %all-reduce.5 = (bf16[128]{0:T(256)(128)(2,1)S(1)}, bf16[128]{0:T(256)(128)(2,1)S(1)}, bf16[128]{0:T(256)(128)(2,1)S(1)}, bf16[128]{0:T(256)(128)(2,1)S(1)}) all-reduce(bf16[128]{0:T(256)(128)(2,1)S(1)} %dynamic-slice.15, bf16[128]{0:T(256)(128)(2,1)S(1)} %dynamic-slice.14, ...), channel_id=1, replica_groups=mesh['dp'=4,'fsdp'=8] {'dp'}, use_global_device_ids=true, to_apply=%region_21.22 | all-reduce | flops 512 | bytes 2048 | tf_op jit(solution)/shard_map/psum | solution.py:229
  863.8 2.4 fusion.52
  866.2 7.9 fusion.31
  874.1 2.6 reduce_sum.168
  878.0 59.2 %all-reduce.9.cloned.1.call-done = (bf16[128,1024]{1,0:T(8,128)(2,1)}, bf16[128,4096]{1,0:T(8,128)(2,1)}, bf16[512,1024]{1,0:T(8,128)(2,1)}) async-done(((bf16[128,1024]{1,0:T(8,128)(2,1)}, bf16[128,4096]{1,0:T(8,128)(2,1)}, bf16[512,1024]{1,0:T(8,128)(2,1)}), (bf16[128,1024]{1,0:T(8,128)(2,1)}, bf16[128,4096]{1,0:T(8,128)(2,1)}, bf16[512,1024]{1,0:T(8,128)(2,1)})) %all-reduce.9.cloned.1.call-update) | async-done | bytes 2359312 | tf_op jit(solution)/shard_map/psum | solution.py:226
  937.2 2.8 convert_element_type.190
  940.0 2.8 convert_element_type.192
  (95 shorter events, 33.9 us)
Async XLA Ops:
  7.2 69.9 %copy-start = (bf16[1,256,1024]{2,1,0:T(8,128)(2,1)S(1)}, bf16[1,256,1024]{2,1,0:T(8,128)(2,1)}, u32[]{:S(2)}) copy-start(bf16[1,256,1024]{2,1,0:T(8,128)(2,1)} %param.11) | copy-start | bytes 1572868
  7.2 69.9 %all-gather.11.cloned.1.call-start = ((), (), s32[]{:S(2)}) async-start(), calls=%async_computation.4 | async-start | bytes 7077888 | tf_op jit(solution)/shard_map/all_gather | solution.py:180
  7.9 98.6 %all-gather.13.cloned.1.call-start = ((), (), s32[]{:S(2)}) async-start(), calls=%async_computation.5 | async-start | bytes 2359296 | tf_op jit(solution)/shard_map/all_gather | solution.py:181
  8.7 180.9 %all-gather.15.cloned.1.call-start = ((), (), s32[]{:S(2)}) async-start(), calls=%async_computation.6 | async-start | bytes 9437184 | tf_op jit(solution)/shard_map/all_gather | solution.py:182
  9.4 262.2 %all-gather.17.cloned.1.call-start = ((), (), s32[]{:S(2)}) async-start(), calls=%async_computation.7 | async-start | bytes 9437184 | tf_op jit(solution)/shard_map/all_gather | solution.py:183
  10.0 416.4 %reduce-scatter.5.cloned.1.call-start = ((), (), s32[]{:S(2)}) async-start(), calls=%async_computation.8 | async-start | bytes 14155776 | tf_op jit(solution)/shard_map/reduce_scatter | solution.py:215
  84.7 2.5 copy-start.1
  87.2 2.0 copy-start.5
  89.6 115.2 %copy-start.9 = (bf16[16,64,256]{2,1,0:T(8,128)(2,1)}, bf16[16,64,256]{2,1,0:T(8,128)(2,1)S(1)}, u32[]{:S(2)}) copy-start(bf16[16,64,256]{2,1,0:T(8,128)(2,1)S(1)} %convolution_convert_fusion.2) | copy-start | bytes 1572868
  189.6 82.0 %copy-start.7 = (bf16[1,256,1024]{2,1,0:T(8,128)(2,1)S(1)}, bf16[1,256,1024]{2,1,0:T(8,128)(2,1)}, u32[]{:S(2)}) copy-start(bf16[1,256,1024]{2,1,0:T(8,128)(2,1)} %param.13) | copy-start | bytes 1572868
  271.6 7.0 copy-start.14
  278.6 2.7 copy-start.11
  278.6 3.1 copy-start.3
  283.5 3.7 copy-start.6
  287.3 1.4 copy-start.2
  288.7 1.2 copy-start.12
  290.9 1.1 copy-start.4
  298.6 1.0 copy-start.10
  298.6 178.3 %reduce-scatter.7.cloned.1.call-start = ((), (), s32[]{:S(2)}) async-start(), calls=%async_computation.9 | async-start | bytes 4718592 | tf_op jit(solution)/shard_map/reduce_scatter | solution.py:216
  302.5 343.5 %reduce-scatter.9.cloned.1.call-start = ((), (), s32[]{:S(2)}) async-start(), calls=%async_computation.10 | async-start | bytes 18874368 | tf_op jit(solution)/shard_map/reduce_scatter | solution.py:217
  313.0 1.0 copy-start.8
  313.1 501.9 %reduce-scatter.11.cloned.1.call-start = ((), (), s32[]{:S(2)}) async-start(), calls=%async_computation.11 | async-start | bytes 18874368 | tf_op jit(solution)/shard_map/reduce_scatter | solution.py:218
  323.9 550.3 %all-gather.19.cloned.1.call-start = ((), (), s32[]{:S(2)}) async-start(), calls=%async_computation.12 | async-start | bytes 3932160 | tf_op jit(solution)/shard_map/all_gather | solution.py:225
  428.8 508.4 %all-reduce.9.cloned.1.call-start = ((), (), s32[]{:S(2)}) async-start(), calls=%async_computation.13 | async-start | bytes 4718592 | tf_op jit(solution)/shard_map/psum | solution.py:226
  478.7 339.0 %copy-start.15 = (u32[32]{0:T(128)S(1)}, u32[32]{0:T(128)}, u32[]{:S(2)}) copy-start(u32[32]{0:T(128)} %constant.91) | copy-start | bytes 388
  937.2 5.6 copy-start.13
Sparse Core Ops, SparseCore 0:
  9.6 67.4 all-gather.10
  78.7 27.7 all-gather.12
  108.1 81.4 all-gather.14
  191.0 80.5 all-gather.16
  298.7 127.6 reduce-scatter.4
  428.5 48.3 reduce-scatter.6
  479.3 166.6 reduce-scatter.8
  648.3 166.6 reduce-scatter.10
  816.8 42.4 all-gather.18
  863.2 73.9 all-reduce.8
